TPU v7x, 32 devices: a whole 2x2x4 slice. The times are simulated.
32 devices in a mesh: trans: 16 (over z, x, core), bin: 2 (over y).
Axes of the slice: x: 2, y: 2, z: 4, core: 2. Of those that a mesh axis runs over, the one named last changes fastest.
Arguments:
- pair_density: bfloat16 [8192, 8000], P('trans', 'bin'), may hold values from -1.5 to 1.5
- bin_index: int32 [8192, 1], P('trans'), may hold values from 0 to 255; in each aligned block of 512 rows (0 to 511, 512 to 1023, ...) at most 4 rows name the same one
- panel_columns: int32 [128], replicated, may hold values from 0 to 7999
Outputs:
- response: float32 [2, 256, 1024000], P(None, None, ('bin', 'trans'))
Inputs may be any that keep to these rules, and one draw needn't show every extreme that they name: `bin_index`: among the 512 transitions of one device no bin occurs more than 4 times, and some bin occurs exactly 4 times. `panel_columns`: entries may repeat.
All inputs are finite; a program needn't handle non-finite values.
Results may differ from a plain program's by a relative error of at most 0.0003.
Values may be sent and summed in bfloat16 or wider, within the bound.
No kernel may reach another device: no remote copies, remote signals or barrier semaphores. Data moves between devices by JAX's collectives and lax.ppermute only.
A program may use at most 256 MiB of HBM per device.

v0:
```python
import jax
import jax.numpy as jnp
from jax import lax
from jax.sharding import PartitionSpec as P

PANEL = 128
NB = 256
MOST = 4
broaden = 1.5


def kernel_tables():
    freq = lax.broadcasted_iota(jnp.int32, (NB,), 0).astype(jnp.float32) + 0.5
    diff = freq[:, None] - freq[None, :]
    total = freq[:, None] + freq[None, :]
    low = diff * diff + broaden * broaden
    high = total * total + broaden * broaden
    return (diff / low - total / high, broaden / high - broaden / low)


def transform(arrived):
    kernel_re, kernel_im = kernel_tables()
    flat = arrived.reshape(arrived.shape[0], arrived.shape[2])
    real_part = jnp.dot(
        kernel_re, flat, precision=lax.Precision.HIGHEST, preferred_element_type=jnp.float32
    )
    imag_part = jnp.dot(
        kernel_im, flat, precision=lax.Precision.HIGHEST, preferred_element_type=jnp.float32
    )
    return jnp.stack([real_part, imag_part])


def local(pair_density, bin_index, panel_columns):
    trans_count = lax.axis_size("trans")
    bin_place = lax.axis_index("bin")
    local_rows, row_count = pair_density.shape
    per_owner = NB // trans_count
    bin_number = bin_index[:, 0]
    matching = bin_number[:, None] == bin_number[None, :]
    earlier = lax.broadcasted_iota(jnp.int32, (local_rows, local_rows), 0) > lax.broadcasted_iota(
        jnp.int32, (local_rows, local_rows), 1
    )
    rank = jnp.sum((matching & earlier).astype(jnp.int32), axis=1)
    slot = bin_number * MOST + rank
    placing = (lax.broadcasted_iota(jnp.int32, (NB * MOST, local_rows), 0) == slot[None, :]).astype(
        jnp.bfloat16
    )
    selector = (
        lax.broadcasted_iota(jnp.int32, (row_count, PANEL), 0) + bin_place * row_count
        == panel_columns[None, :]
    ).astype(jnp.bfloat16)
    send_rows = jnp.dot(placing, pair_density, preferred_element_type=jnp.float32).astype(
        jnp.bfloat16
    )
    got_rows = lax.all_to_all(send_rows, "trans", split_axis=0, concat_axis=0, tiled=True)
    got_panel = lax.psum(
        jnp.dot(got_rows, selector, preferred_element_type=jnp.float32).astype(jnp.bfloat16), "bin"
    )
    rows_split = got_rows.reshape(trans_count, per_owner, MOST, row_count)
    panel_split = got_panel.reshape(trans_count, per_owner, MOST, PANEL)
    spectral = jnp.einsum(
        "sbmg,sbmc->bgc", rows_split, panel_split, preferred_element_type=jnp.float32
    )
    piece_width = row_count * PANEL // trans_count
    slab = spectral.reshape(per_owner, trans_count, piece_width)
    arrived = lax.all_to_all(slab, "trans", split_axis=1, concat_axis=0, tiled=True)
    response = transform(arrived)
    return response


def solution(mesh):
    placed = (P("trans", "bin"), P("trans", None), P())
    return jax.shard_map(
        local,
        mesh=mesh,
        in_specs=placed,
        out_specs=P(None, None, ("bin", "trans")),
        check_vma=False,
    )
```

profile of v0, /device:TPU:11, one launch (start us, length us, event | category | flops | bytes accessed | tf_op | source)
XLA Modules:
  0.0 1157.1 jit_solution(17632754684267863969)
XLA Ops:
  6.5 0.0 copy-start
  6.5 1.0 convert_reduce_fusion
  7.5 0.7 multiply_add_fusion
  8.2 8.9 convolution_convert_fusion
  17.1 11.7 %copy.10 = bf16[1024,4000]{1,0:T(8,128)(2,1)} copy(bf16[1024,4000]{0,1:T(8,128)(2,1)} %convolution_convert_fusion) | data formatting | bytes 16384000 | tf_op jit(solution)/shard_map/convert_element_type | solution.py:52
  28.8 6.5 all-to-all-start
  35.4 0.2 all-reduce.2.cloned.1.call-start
  35.6 182.1 %all-to-all-done = bf16[16,64,4000]{2,1,0:T(8,128)(2,1)} async-done(((bf16[16,64,4000]{2,1,0:T(8,128)(2,1)}), bf16[16,64,4000]{2,1,0:T(8,128)(2,1)}, u32[]{:S(2)}, u32[]{:S(2)}) %all-to-all-start) | async-done | bytes 8192032 | tf_op jit(solution)/shard_map/all_to_all | solution.py:55
  217.7 0.0 copy-done
  217.7 5.8 fusion.2
  223.5 0.9 copy.12
  224.4 0.0 all-reduce.2.cloned.1.call-update
  224.4 11.2 copy.11
  235.6 11.2 all-reduce.2.cloned.1.call-done
  246.8 16.1 %convolution_bitcast_fusion.2 = f32[16,4000,128]{2,1,0:T(8,128)} fusion(bf16[16,16,4,4000]{3,0,2,1:T(8,128)(2,1)} %bitcast.24, bf16[16,16,4,128]{3,0,2,1:T(8,128)(2,1)} %all-reduce.2.cloned.1.call-done), kind=kOutput, calls=%fused_computation.3 | convolution fusion | flops 1048576000 | bytes 41222144 | tf_op jit(solution)/shard_map/sbmg,sbmc->bgc/dot_general | solution.py:61
  263.0 29.6 %reshape.38 = f32[16,16,32000]{2,1,0:T(8,128)} reshape(f32[16,4000,128]{2,1,0:T(8,128)} %convolution_bitcast_fusion.2) | data formatting | bytes 65536000 | tf_op jit(solution)/shard_map/reshape | solution.py:65
  292.6 27.4 %copy.13 = f32[16,16,32000]{2,0,1:T(8,128)} copy(f32[16,16,32000]{2,1,0:T(8,128)} %reshape.38) | data formatting | bytes 65536000 | tf_op jit(solution)/shard_map/reshape | solution.py:65
  320.0 7.2 all-to-all-start.1
  327.3 704.8 %all-to-all-done.1 = f32[16,16,32000]{2,0,1:T(8,128)} async-done(((f32[16,16,32000]{2,0,1:T(8,128)}), f32[16,16,32000]{2,0,1:T(8,128)}, u32[]{:S(2)}, u32[]{:S(2)}) %all-to-all-start.1) | async-done | bytes 32768032 | tf_op jit(solution)/shard_map/all_to_all | solution.py:66
  1032.1 37.1 %convolution_bitcast_fusion = f32[1,256,32000]{2,1,0:T(8,128)} fusion(f32[256,32000]{1,0:T(8,128)} %bitcast.9, f32[256]{0:T(256)S(1)} %convert_add_fusion), kind=kOutput, calls=%fused_computation.1 | convolution fusion | flops 25166413824 | bytes 65537024 | tf_op jit(solution)/shard_map/dot_general | solution.py:27
  1069.1 37.1 %convolution_bitcast_fusion.1 = f32[1,256,32000]{2,1,0:T(8,128)} fusion(f32[256,32000]{1,0:T(8,128)} %bitcast.9, f32[256]{0:T(256)S(1)} %convert_add_fusion), kind=kOutput, calls=%fused_computation.2 | convolution fusion | flops 25166413824 | bytes 65537024 | tf_op jit(solution)/shard_map/dot_general | solution.py:24
  1106.3 43.9 %pad_maximum_fusion = f32[2,256,32000]{2,1,0:T(8,128)} fusion(f32[1,256,32000]{2,1,0:T(8,128)} %convolution_bitcast_fusion, f32[1,256,32000]{2,1,0:T(8,128)} %convolution_bitcast_fusion.1), kind=kLoop, calls=%fused_computation | loop fusion | flops 16384000 | bytes 131072000 | tf_op jit(solution)/shard_map/stack | solution.py:30
  (2 shorter events, 0.0 us)
Async XLA Ops:
  6.5 211.2 %copy-start = (s32[128]{0:T(128)S(1)}, s32[128]{0:T(128)}, u32[]{:S(2)}) copy-start(s32[128]{0:T(128)} %param.5) | copy-start | bytes 1540
  28.8 188.9 %all-to-all-start = ((bf16[16,64,4000]{2,1,0:T(8,128)(2,1)}), bf16[16,64,4000]{2,1,0:T(8,128)(2,1)}, u32[]{:S(2)}, u32[]{:S(2)}) async-start(bf16[16,64,4000]{2,1,0:T(8,128)(2,1)} %bitcast.23), calls=%async_computation | async-start | bytes 16777216 | tf_op jit(solution)/shard_map/all_to_all | solution.py:55
  35.4 211.4 %all-reduce.2.cloned.1.call-start = ((), (), s32[]{:S(2)}) async-start(), calls=%async_computation.2 | async-start | bytes 524288 | tf_op jit(solution)/shard_map/psum | solution.py:56
  320.0 712.0 %all-to-all-start.1 = ((f32[16,16,32000]{2,0,1:T(8,128)}), f32[16,16,32000]{2,0,1:T(8,128)}, u32[]{:S(2)}, u32[]{:S(2)}) async-start(f32[16,16,32000]{2,0,1:T(8,128)} %copy.13), calls=%async_computation.1 | async-start | bytes 65536000 | tf_op jit(solution)/shard_map/all_to_all | solution.py:66
Sparse Core Ops, SparseCore 0:
  224.6 22.2 all-reduce.1
where the time goes:
time: 1160 us
  waiting for transfers between devices  898 us (77%)
  matrix products  105 us (9%)
  local copies, waits for them, and re-layouts  80.8 us (7%)
  other arithmetic  45.6 us (4%)
  starting transfers between devices  14 us (1%)
  between operations  13.4 us (1%)
    all_to_all x1, waiting for transfers between devices, local(): lax.all_to_all(slab, 'trans', split_axis=1, concat_axis=0, tiled=True)  705 us
    all_to_all x1, waiting for transfers between devices, local(): lax.all_to_all(send_rows, 'trans', split_axis=0, concat_axis=0, tiled=True)  182 us
    reshape x2, local copies, waits for them, and re-layouts, local(): slab = spectral.reshape(per_owner, trans_count, piece_width)  57.1 us
    another operation x1, other arithmetic, transform(): return jnp.stack([real_part, imag_part])  43.9 us
    dot_general x1, matrix products, transform(): jnp.dot(kernel_re, flat, precision=lax.Precision.HIGHEST, preferred_eleme...  37.1 us
    dot_general x1, matrix products, transform(): jnp.dot(kernel_im, flat, precision=lax.Precision.HIGHEST, preferred_eleme...  37.1 us
  transfers between devices with their start and end apart: 3, of which 3 were waited for; matrix products, arithmetic and copies ran while one was open for 1% of the time, Pallas kernels for 0%

commit v1 on v0

--- a/solution.py
+++ b/solution.py
@@ -1,3 +1,4 @@
+import functools
 import jax
 import jax.numpy as jnp
 from jax import lax
@@ -7,6 +8,21 @@
 NB = 256
 MOST = 4
 broaden = 1.5
+
+
+def core_load(local_array, link_axis):
+    return jnp.concatenate(
+        lax.all_to_all(
+            jnp.stack(jnp.split(local_array, lax.axis_size(link_axis), axis=1), axis=0),
+            axis_name=link_axis,
+            split_axis=0,
+            concat_axis=0,
+        ),
+        axis=0,
+    )
+
+
+do_the_axis_part = functools.partial(core_load, link_axis="trans")
 
 
 def kernel_tables():
@@ -63,7 +79,7 @@
     )
     piece_width = row_count * PANEL // trans_count
     slab = spectral.reshape(per_owner, trans_count, piece_width)
-    arrived = lax.all_to_all(slab, "trans", split_axis=1, concat_axis=0, tiled=True)
+    arrived = do_the_axis_part(slab)
     response = transform(arrived)
     return response
 

time: 1160 us -> 1300 us (1.12)
  local copies, waits for them, and re-layouts: 80.8 us -> 217 us
    unnamed x2 -> x18, local copies, waits for them, and re-layouts: 0.01 us -> 155 us
    reshape x2 -> x1, local copies, waits for them, and re-layouts: 57.1 us -> 30 us  [local(): slab = spectral.reshape(per_owner, trans_count, piece_width)]
where the time goes in v1:
time: 1300 us; the launch traced here: 1290 us
  waiting for transfers between devices  898 us (69%)
  local copies, waits for them, and re-layouts  217 us (17%)
  matrix products  105 us (8%)
  other arithmetic  45.6 us (4%)
  between operations  13.9 us (1%)
  starting transfers between devices  13.8 us (1%)
    all_to_all x1, waiting for transfers between devices, core_load(): lax.all_to_all(jnp.stack(jnp.split(local_array, lax.axis_size(link_axis),...  705 us
    all_to_all x1, waiting for transfers between devices, local(): lax.all_to_all(send_rows, 'trans', split_axis=0, concat_axis=0, tiled=True)  182 us
    unnamed x18, local copies, waits for them, and re-layouts  155 us
    another operation x1, other arithmetic, transform(): return jnp.stack([real_part, imag_part])  43.9 us
    dot_general x1, matrix products, transform(): jnp.dot(kernel_re, flat, precision=lax.Precision.HIGHEST, preferred_eleme...  37.3 us
    dot_general x1, matrix products, transform(): jnp.dot(kernel_im, flat, precision=lax.Precision.HIGHEST, preferred_eleme...  37 us
    reshape x1, local copies, waits for them, and re-layouts, local(): slab = spectral.reshape(per_owner, trans_count, piece_width)  30 us
  transfers between devices with their start and end apart: 3, of which 3 were waited for; matrix products, arithmetic and copies ran while one was open for 1% of the time, Pallas kernels for 0%

profile of v1, /device:TPU:11, one launch (start us, length us, event | category | flops | bytes accessed | tf_op | source)
XLA Modules:
  0.0 1293.7 jit_solution(4786889394883764445)
XLA Ops:
  6.5 0.0 copy-start
  6.5 1.0 convert_reduce_fusion
  7.5 0.7 multiply_add_fusion
  8.2 8.9 convolution_convert_fusion
  17.2 11.7 copy.9
  28.9 6.5 all-to-all-start
  35.4 0.2 all-reduce.2.cloned.1.call-start
  35.6 182.1 %all-to-all-done = bf16[16,64,4000]{2,1,0:T(8,128)(2,1)} async-done(((bf16[16,64,4000]{2,1,0:T(8,128)(2,1)}), bf16[16,64,4000]{2,1,0:T(8,128)(2,1)}, u32[]{:S(2)}, u32[]{:S(2)}) %all-to-all-start) | async-done | bytes 8192032 | tf_op jit(solution)/shard_map/all_to_all | solution.py:71
  217.7 0.0 copy-done
  217.7 5.8 fusion.18
  223.5 0.9 copy.11
  224.4 0.0 all-reduce.2.cloned.1.call-update
  224.4 11.2 copy.10
  235.6 11.2 all-reduce.2.cloned.1.call-done
  246.8 16.1 %convolution_bitcast_fusion.2 = f32[16,4000,128]{2,1,0:T(8,128)} fusion(bf16[16,16,4,4000]{3,0,2,1:T(8,128)(2,1)} %bitcast.86, bf16[16,16,4,128]{3,0,2,1:T(8,128)(2,1)} %all-reduce.2.cloned.1.call-done), kind=kOutput, calls=%fused_computation.3 | convolution fusion | flops 1048576000 | bytes 41222144 | tf_op jit(solution)/shard_map/sbmg,sbmc->bgc/dot_general | solution.py:77
  263.0 30.0 %reshape.34 = f32[16,16,32000]{2,1,0:T(8,128)} reshape(f32[16,4000,128]{2,1,0:T(8,128)} %convolution_bitcast_fusion.2) | data formatting | bytes 65536000 | tf_op jit(solution)/shard_map/reshape | solution.py:81
  293.0 8.0 fusion.15
  301.0 8.7 fusion.14
  309.7 8.7 fusion.13
  318.4 8.7 fusion.12
  327.1 8.7 fusion.11
  335.9 8.7 fusion.10
  344.6 8.9 fusion.9
  353.4 8.7 fusion.8
  362.2 8.0 fusion.7
  370.2 8.7 fusion.6
  378.9 8.7 fusion.5
  387.6 8.7 fusion.4
  396.3 8.7 fusion.3
  405.0 8.9 fusion.2
  413.9 8.7 fusion.1
  422.6 8.7 fusion
  431.4 7.0 all-to-all-start.1
  438.4 704.8 %all-to-all-done.1 = f32[16,16,1,32000]{3,2,1,0:T(1,128)} async-done(((f32[16,16,1,32000]{3,2,1,0:T(1,128)}), f32[16,16,1,32000]{3,2,1,0:T(1,128)}, u32[]{:S(2)}, u32[]{:S(2)}) %all-to-all-start.1) | async-done | bytes 32768032 | tf_op jit(solution)/shard_map/all_to_all | solution.py:15
  1143.2 25.0 %copy.13 = f32[16,16,1,32000]{3,1,2,0:T(8,128)} copy(f32[16,16,1,32000]{3,2,1,0:T(1,128)} %all-to-all-done.1) | data formatting | bytes 65536000
  1168.1 37.0 %convolution_bitcast_fusion = f32[1,256,32000]{2,1,0:T(8,128)} fusion(f32[256,32000]{1,0:T(8,128)} %bitcast.83, f32[256]{0:T(256)S(1)} %convert_add_fusion), kind=kOutput, calls=%fused_computation.1 | convolution fusion | flops 25166413824 | bytes 65537024 | tf_op jit(solution)/shard_map/dot_general | solution.py:43
  1205.2 37.3 %convolution_bitcast_fusion.1 = f32[1,256,32000]{2,1,0:T(8,128)} fusion(f32[256,32000]{1,0:T(8,128)} %bitcast.84, f32[256]{0:T(256)S(1)} %convert_add_fusion), kind=kOutput, calls=%fused_computation.2 | convolution fusion | flops 25166413824 | bytes 65537024 | tf_op jit(solution)/shard_map/dot_general | solution.py:40
  1242.5 43.9 %pad_maximum_fusion = f32[2,256,32000]{2,1,0:T(8,128)} fusion(f32[1,256,32000]{2,1,0:T(8,128)} %convolution_bitcast_fusion, f32[1,256,32000]{2,1,0:T(8,128)} %convolution_bitcast_fusion.1), kind=kLoop, calls=%fused_computation | loop fusion | flops 16384000 | bytes 131072000 | tf_op jit(solution)/shard_map/stack | solution.py:46
  (2 shorter events, 0.0 us)
Async XLA Ops:
  6.5 211.2 %copy-start = (s32[128]{0:T(128)S(1)}, s32[128]{0:T(128)}, u32[]{:S(2)}) copy-start(s32[128]{0:T(128)} %param.5) | copy-start | bytes 1540
  28.9 188.9 %all-to-all-start = ((bf16[16,64,4000]{2,1,0:T(8,128)(2,1)}), bf16[16,64,4000]{2,1,0:T(8,128)(2,1)}, u32[]{:S(2)}, u32[]{:S(2)}) async-start(bf16[16,64,4000]{2,1,0:T(8,128)(2,1)} %bitcast.85), calls=%async_computation | async-start | bytes 16777216 | tf_op jit(solution)/shard_map/all_to_all | solution.py:71
  35.4 211.5 %all-reduce.2.cloned.1.call-start = ((), (), s32[]{:S(2)}) async-start(), calls=%async_computation.2 | async-start | bytes 524288 | tf_op jit(solution)/shard_map/psum | solution.py:72
  431.4 711.8 %all-to-all-start.1 = ((f32[16,16,1,32000]{3,2,1,0:T(1,128)}), f32[16,16,1,32000]{3,2,1,0:T(1,128)}, u32[]{:S(2)}, u32[]{:S(2)}) async-start(f32[16,16,1,32000]{3,2,1,0:T(1,128)} %fusion), calls=%async_computation.1 | async-start | bytes 65536000 | tf_op jit(solution)/shard_map/all_to_all | solution.py:15
Sparse Core Ops, SparseCore 0:
  224.6 22.2 all-reduce.1
